TPU v7x, 32 devices: a whole 2x2x4 slice. The times are simulated.
32 devices in a mesh: energy: 8 (over z, y), cell: 4 (over x, core).
Axes of the slice: x: 2, y: 2, z: 4, core: 2. Of those that a mesh axis runs over, the one named last changes fastest.
Arguments:
- g_lesser: float32 [2, 8, 4, 256, 256], P(None, 'energy', 'cell'), may hold values from -6 to 6
- g_greater: float32 [2, 8, 4, 256, 256], P(None, 'energy', 'cell'), may hold values from -6 to 6
- w_diag: float32 [2, 8, 4, 256, 256], P(None, 'energy', 'cell'), may hold values from -0.25 to 0.25
- w_upper: float32 [2, 8, 4, 256, 256], P(None, 'energy', 'cell'), may hold values from -0.25 to 0.25
- coupled: int32 [4], P('cell'), may hold values from 1 to 16
Outputs:
- polarization: float32 [2, 8, 4, 256, 256], P(None, 'energy', 'cell')
- screened: float32 [2, 8, 4, 256, 256], P(None, 'energy', 'cell')
All inputs are finite; a program needn't handle non-finite values.
Results may differ from a plain program's by a relative error of at most 0.0003.
Values sent between devices are 32-bit elements; how exact they have to be, the bound alone decides.
A program may use at most 64 MiB of HBM per device.

v0:
```python
import math

import jax
import jax.numpy as jnp
from jax import lax
from jax.sharding import PartitionSpec as P


def shifted(shard, axis, by):
    size = lax.axis_size(axis)
    pairs = [(i, i + by) for i in range(size) if 0 <= i + by < size]
    return lax.ppermute(shard, axis, pairs)


def complex_product(left, right):

    def matmul(first, second):
        return jnp.einsum("...ij,...jk->...ik", first, second, precision=lax.Precision.HIGHEST)

    real = matmul(left[0], right[0]) - matmul(left[1], right[1])
    imaginary = matmul(left[0], right[1]) + matmul(left[1], right[0])
    return jnp.stack([real, imaginary])


def adjoint(block):
    return jnp.stack([jnp.swapaxes(block[0], -1, -2), -jnp.swapaxes(block[1], -1, -2)])


def transposed(block):
    return jnp.stack([jnp.swapaxes(block[0], -1, -2), jnp.swapaxes(block[1], -1, -2)])


def conjugate(block):
    return jnp.stack([block[0], -block[1]])


def transform(table, data):
    return jnp.dot(table, data, preferred_element_type=jnp.float32, precision=lax.Precision.HIGHEST)


def convolve(pieces):
    lesser_part, greater_part = pieces
    piece_shape = lesser_part.shape
    energies = piece_shape[1]
    padded_length = 2 * energies
    lesser_flat = lesser_part.reshape(2, energies, -1)
    greater_flat = greater_part.reshape(2, energies, -1)
    frequency = jnp.arange(padded_length, dtype=jnp.int32)
    points = jnp.arange(energies, dtype=jnp.int32)
    phases = (frequency[:, None] * points[None, :] % padded_length).astype(jnp.float32) * (
        2.0 * math.pi / padded_length
    )
    cosines = jnp.cos(phases)
    sines = jnp.sin(phases)
    lesser_real = transform(cosines, lesser_flat[0]) + transform(sines, lesser_flat[1])
    lesser_imaginary = transform(cosines, lesser_flat[1]) - transform(sines, lesser_flat[0])
    greater_real = transform(cosines, greater_flat[0]) - transform(sines, greater_flat[1])
    greater_imaginary = transform(cosines, greater_flat[1]) + transform(sines, greater_flat[0])
    product_real = lesser_real * greater_real - lesser_imaginary * greater_imaginary
    product_imaginary = lesser_real * greater_imaginary + lesser_imaginary * greater_real
    back_cosines = cosines.T
    back_sines = sines.T
    back_real = transform(back_cosines, product_real) - transform(back_sines, product_imaginary)
    back_imaginary = transform(back_cosines, product_imaginary) + transform(
        back_sines, product_real
    )
    factor = 1.0 / (padded_length * math.sqrt(energies))
    polar_piece = jnp.stack([back_imaginary * factor, -back_real * factor]).reshape(piece_shape)
    return lax.all_to_all(polar_piece, "energy", split_axis=1, concat_axis=3, tiled=True)


def body(g_lesser, g_greater, w_diag, w_upper, coupled):
    greater_t = jnp.swapaxes(g_greater, 3, 4)
    polarization = convolve(
        (
            lax.all_to_all(g_lesser, "energy", split_axis=3, concat_axis=1, tiled=True),
            lax.all_to_all(greater_t, "energy", split_axis=3, concat_axis=1, tiled=True),
        )
    )
    coupling = (coupled.astype(g_lesser.dtype) * 0.125)[None, None, :, None, None]
    upper_block = w_upper * coupling
    above_polar = shifted(polarization, "cell", -1)
    next_polar = jnp.concatenate([polarization[:, :, 1:], above_polar], axis=2)
    own_term = complex_product(complex_product(w_diag, polarization), adjoint(w_diag))
    upper_term = complex_product(complex_product(upper_block, next_polar), adjoint(upper_block))
    below_polar, below_upper = shifted((polarization, upper_block), "cell", 1)
    prev_polar = jnp.concatenate([below_polar, polarization[:, :, :-1]], axis=2)
    prev_upper = jnp.concatenate([below_upper, upper_block[:, :, :-1]], axis=2)
    lower_term = complex_product(
        complex_product(transposed(prev_upper), prev_polar), conjugate(prev_upper)
    )
    return (polarization, own_term + upper_term + lower_term)


def solution(mesh):
    return jax.shard_map(
        body,
        mesh=mesh,
        in_specs=(
            P(None, "energy", "cell", None, None),
            P(None, "energy", "cell", None, None),
            P(None, "energy", "cell", None, None),
            P(None, "energy", "cell", None, None),
            P("cell"),
        ),
        out_specs=(P(None, "energy", "cell", None, None), P(None, "energy", "cell", None, None)),
        check_vma=False,
    )
```

profile of v0, /device:TPU:1, one launch (start us, length us, event | category | flops | bytes accessed | tf_op | source)
XLA Modules:
  0.0 91.1 jit_solution(1159953040156037103)
XLA Ops:
  0.6 2.2 %copy.27 = f32[2,1,1,256,256]{4,0,2,1,3:T(2,128)} copy(f32[2,1,1,256,256]{4,3,2,1,0:T(8,128)} %param.5) | data formatting | bytes 1048576 | tf_op args[0]
  2.9 6.5 %all-to-all-start = ((f32[2,1,1,256,256]{4,0,2,1,3:T(2,128)}), f32[2,1,1,256,256]{4,0,2,1,3:T(2,128)S(1)}, u32[]{:S(2)}, u32[]{:S(2)}) async-start(f32[2,1,1,256,256]{4,0,2,1,3:T(2,128)} %copy.27), calls=%async_computation | async-start | bytes 1048576 | tf_op jit(solution)/shard_map/all_to_all | solution.py:76
  9.4 1.0 %copy.28 = f32[2,1,1,256,256]{3,2,1,0,4:T(1,128)} copy(f32[2,1,1,256,256]{4,3,2,1,0:T(8,128)S(1)} %copy-done.1) | data formatting | bytes 1048576 | tf_op args[1]
  10.4 12.4 %all-to-all-done = f32[2,1,1,256,256]{4,0,2,1,3:T(2,128)S(1)} async-done(((f32[2,1,1,256,256]{4,0,2,1,3:T(2,128)}), f32[2,1,1,256,256]{4,0,2,1,3:T(2,128)S(1)}, u32[]{:S(2)}, u32[]{:S(2)}) %all-to-all-start) | async-done | bytes 524320 | tf_op jit(solution)/shard_map/all_to_all | solution.py:76
  22.8 4.9 %all-to-all-start.1 = ((f32[2,1,1,256,256]{4,2,1,0,3:T(1,128)}), f32[2,1,1,256,256]{4,2,1,0,3:T(1,128)S(1)}, u32[]{:S(2)}, u32[]{:S(2)}) async-start(f32[2,1,1,256,256]{4,2,1,0,3:T(1,128)} %bitcast), calls=%async_computation.1 | async-start | bytes 1048576 | tf_op jit(solution)/shard_map/all_to_all | solution.py:77
  27.7 1.3 %slice_reduce_fusion.3 = (f32[256,256]{1,0:T(8,128)S(1)}, f32[256,256]{1,0:T(8,128)S(1)}) fusion(f32[2,1,1,256,256]{4,0,2,1,3:T(2,128)S(1)} %all-to-all-done), kind=kLoop, calls=%fused_computation.41 | loop fusion | bytes 1048576 | tf_op jit(solution)/shard_map/slice | solution.py:55
  29.1 0.6 fusion.74
  29.8 0.6 fusion.78
  30.4 0.6 convolution_add_fusion.1
  31.0 10.2 %all-to-all-done.1 = f32[2,1,1,256,256]{4,2,1,0,3:T(1,128)S(1)} async-done(((f32[2,1,1,256,256]{4,2,1,0,3:T(1,128)}), f32[2,1,1,256,256]{4,2,1,0,3:T(1,128)S(1)}, u32[]{:S(2)}, u32[]{:S(2)}) %all-to-all-start.1) | async-done | bytes 524320 | tf_op jit(solution)/shard_map/all_to_all | solution.py:77
  41.2 1.3 %slice_reduce_fusion = (f32[256,256]{1,0:T(8,128)S(1)}, f32[256,256]{1,0:T(8,128)S(1)}) fusion(f32[2,1,1,256,256]{4,2,1,0,3:T(1,128)S(1)} %all-to-all-done.1), kind=kLoop, calls=%fused_computation.38 | loop fusion | bytes 1048576 | tf_op jit(solution)/shard_map/slice | solution.py:58
  42.6 0.6 fusion.76
  43.3 0.6 fusion.72
  43.9 0.6 convolution_add_fusion
  44.5 0.6 convolution_subtract_fusion
  45.2 0.7 multiply_add_fusion
  48.0 0.8 pad_maximum_fusion
  48.9 4.9 %all-to-all-start.2 = ((f32[2,8,1,32,256]{4,3,2,0,1:T(8,128)}), f32[2,8,1,32,256]{4,3,2,0,1:T(8,128)S(1)}, u32[]{:S(2)}, u32[]{:S(2)}) async-start(f32[2,8,1,32,256]{4,3,2,0,1:T(8,128)} %pad_maximum_fusion), calls=%async_computation.2 | async-start | bytes 1048576 | tf_op jit(solution)/shard_map/all_to_all | solution.py:69
  54.5 3.8 %collective-permute-start.1 = (f32[2,1,1,256,256]{4,3,2,1,0:T(8,128)S(1)}, f32[2,1,1,256,256]{4,3,2,1,0:T(8,128)S(1)}, u32[]{:S(2)}, u32[]{:S(2)}) collective-permute-start(f32[2,1,1,256,256]{4,3,2,1,0:T(8,128)S(1)} %broadcast_multiply_fusion), channel_id=1, source_target_pairs={{0,1},{1,2},{2,3},{4,5},{5,6},{6,7},{8,9},{9,10},{10,11},{12,13},{... | collective-permute-start | bytes 1572872 | tf_op jit(solution)/shard_map/ppermute | solution.py:12
  58.3 9.0 %all-to-all-done.2 = f32[2,8,1,32,256]{4,3,2,0,1:T(8,128)S(1)} async-done(((f32[2,8,1,32,256]{4,3,2,0,1:T(8,128)}), f32[2,8,1,32,256]{4,3,2,0,1:T(8,128)S(1)}, u32[]{:S(2)}, u32[]{:S(2)}) %all-to-all-start.2) | async-done | bytes 524320 | tf_op jit(solution)/shard_map/all_to_all | solution.py:69
  67.4 5.1 %collective-permute-start.2 = (f32[2,1,1,256,256]{4,3,0,2,1:T(8,128)S(1)}, f32[2,1,1,256,256]{4,3,0,2,1:T(8,128)S(1)}, u32[]{:S(2)}, u32[]{:S(2)}) collective-permute-start(f32[2,1,1,256,256]{4,3,0,2,1:T(8,128)S(1)} %bitcast.134), channel_id=1, source_target_pairs={{0,1},{1,2},{2,3},{4,5},{5,6},{6,7},{8,9},{9,10},{10,11},{12,13},{... | collective-permute-start | bytes 1572872 | tf_op jit(solution)/shard_map/ppermute | solution.py:12
  72.4 2.1 %collective-permute-start = (f32[2,1,1,256,256]{4,3,0,2,1:T(8,128)S(1)}, f32[2,1,1,256,256]{4,3,0,2,1:T(8,128)S(1)}, u32[]{:S(2)}, u32[]{:S(2)}) collective-permute-start(f32[2,1,1,256,256]{4,3,0,2,1:T(8,128)S(1)} %bitcast.135), channel_id=1, source_target_pairs={{1,0},{2,1},{3,2},{5,4},{6,5},{7,6},{9,8},{10,9},{11,10},{13,12},{... | collective-permute-start | bytes 1572872 | tf_op jit(solution)/shard_map/ppermute | solution.py:12
  79.4 3.5 %collective-permute-done = f32[2,1,1,256,256]{4,3,0,2,1:T(8,128)S(1)} collective-permute-done((f32[2,1,1,256,256]{4,3,0,2,1:T(8,128)S(1)}, f32[2,1,1,256,256]{4,3,0,2,1:T(8,128)S(1)}, u32[]{:S(2)}, u32[]{:S(2)}) %collective-permute-start) | collective-permute-done | bytes 524320 | tf_op jit(solution)/shard_map/ppermute | solution.py:12
  90.2 0.9 fusion.9
  (47 shorter events, 14.3 us)
Async XLA Ops:
  2.9 6.5 %copy-start.1 = (f32[2,1,1,256,256]{4,3,2,1,0:T(8,128)S(1)}, f32[2,1,1,256,256]{4,3,2,1,0:T(8,128)}, u32[]{:S(2)}) copy-start(f32[2,1,1,256,256]{4,3,2,1,0:T(8,128)} %param.6) | copy-start | bytes 1572868
  2.9 19.9 %all-to-all-start = ((f32[2,1,1,256,256]{4,0,2,1,3:T(2,128)}), f32[2,1,1,256,256]{4,0,2,1,3:T(2,128)S(1)}, u32[]{:S(2)}, u32[]{:S(2)}) async-start(f32[2,1,1,256,256]{4,0,2,1,3:T(2,128)} %copy.27), calls=%async_computation | async-start | bytes 1048576 | tf_op jit(solution)/shard_map/all_to_all | solution.py:76
  22.8 18.4 %all-to-all-start.1 = ((f32[2,1,1,256,256]{4,2,1,0,3:T(1,128)}), f32[2,1,1,256,256]{4,2,1,0,3:T(1,128)S(1)}, u32[]{:S(2)}, u32[]{:S(2)}) async-start(f32[2,1,1,256,256]{4,2,1,0,3:T(1,128)} %bitcast), calls=%async_computation.1 | async-start | bytes 1048576 | tf_op jit(solution)/shard_map/all_to_all | solution.py:77
  48.9 5.6 %copy-start.3 = (f32[2,1,1,256,256]{4,3,2,1,0:T(8,128)S(1)}, f32[2,1,1,256,256]{4,3,2,1,0:T(8,128)}, u32[]{:S(2)}) copy-start(f32[2,1,1,256,256]{4,3,2,1,0:T(8,128)} %param.8) | copy-start | bytes 1572868
  48.9 18.4 %all-to-all-start.2 = ((f32[2,8,1,32,256]{4,3,2,0,1:T(8,128)}), f32[2,8,1,32,256]{4,3,2,0,1:T(8,128)S(1)}, u32[]{:S(2)}, u32[]{:S(2)}) async-start(f32[2,8,1,32,256]{4,3,2,0,1:T(8,128)} %pad_maximum_fusion), calls=%async_computation.2 | async-start | bytes 1048576 | tf_op jit(solution)/shard_map/all_to_all | solution.py:69
  54.5 31.7 %collective-permute-start.1 = (f32[2,1,1,256,256]{4,3,2,1,0:T(8,128)S(1)}, f32[2,1,1,256,256]{4,3,2,1,0:T(8,128)S(1)}, u32[]{:S(2)}, u32[]{:S(2)}) collective-permute-start(f32[2,1,1,256,256]{4,3,2,1,0:T(8,128)S(1)} %broadcast_multiply_fusion), channel_id=1, source_target_pairs={{0,1},{1,2},{2,3},{4,5},{5,6},{6,7},{8,9},{9,10},{10,11},{12,13},{... | collective-permute-start | bytes 1572872 | tf_op jit(solution)/shard_map/ppermute | solution.py:12
  67.3 7.2 %copy-start.2 = (f32[2,8,1,32,256]{4,3,1,0,2:T(8,128)}, f32[2,8,1,32,256]{4,3,1,0,2:T(8,128)S(1)}, u32[]{:S(2)}) copy-start(f32[2,8,1,32,256]{4,3,1,0,2:T(8,128)S(1)} %copy.31) | copy-start | bytes 1572868
  67.4 7.2 %copy-start = (f32[2,1,1,256,256]{4,3,2,1,0:T(8,128)S(1)}, f32[2,1,1,256,256]{4,3,2,1,0:T(8,128)}, u32[]{:S(2)}) copy-start(f32[2,1,1,256,256]{4,3,2,1,0:T(8,128)} %param.7) | copy-start | bytes 1572868
  67.4 18.8 %collective-permute-start.2 = (f32[2,1,1,256,256]{4,3,0,2,1:T(8,128)S(1)}, f32[2,1,1,256,256]{4,3,0,2,1:T(8,128)S(1)}, u32[]{:S(2)}, u32[]{:S(2)}) collective-permute-start(f32[2,1,1,256,256]{4,3,0,2,1:T(8,128)S(1)} %bitcast.134), channel_id=1, source_target_pairs={{0,1},{1,2},{2,3},{4,5},{5,6},{6,7},{8,9},{9,10},{10,11},{12,13},{... | collective-permute-start | bytes 1572872 | tf_op jit(solution)/shard_map/ppermute | solution.py:12
  72.4 10.5 %collective-permute-start = (f32[2,1,1,256,256]{4,3,0,2,1:T(8,128)S(1)}, f32[2,1,1,256,256]{4,3,0,2,1:T(8,128)S(1)}, u32[]{:S(2)}, u32[]{:S(2)}) collective-permute-start(f32[2,1,1,256,256]{4,3,0,2,1:T(8,128)S(1)} %bitcast.135), channel_id=1, source_target_pairs={{1,0},{2,1},{3,2},{5,4},{6,5},{7,6},{9,8},{10,9},{11,10},{13,12},{... | collective-permute-start | bytes 1572872 | tf_op jit(solution)/shard_map/ppermute | solution.py:12
where the time goes:
time: 91.6 us; the launch traced here: 91.1 us
  waiting for transfers between devices  35.1 us (38%)
  starting transfers between devices  27.2 us (30%)
  matrix products  18.8 us (21%)
  local copies, waits for them, and re-layouts  6.42 us (7%)
  other arithmetic  1.77 us (2%)
  between operations  1.73 us (2%)
    all_to_all x1, waiting for transfers between devices, body(): lax.all_to_all(g_lesser, 'energy', split_axis=3, concat_axis=1, tiled=True)  12.4 us
    dot_general x24, matrix products, matmul(): jnp.einsum('...ij,...jk->...ik', first, second, precision=lax.Precision.H...  11.9 us
    ppermute x3, starting transfers between devices, shifted(): return lax.ppermute(shard, axis, pairs)  10.9 us
    all_to_all x1, waiting for transfers between devices, body(): lax.all_to_all(greater_t, 'energy', split_axis=3, concat_axis=1, tiled=True)  10.2 us
    all_to_all x1, waiting for transfers between devices, convolve(): lax.all_to_all(polar_piece, 'energy', split_axis=1, concat_axis=3, tiled=...  9.03 us
    dot_general x12, matrix products, transform(): jnp.dot(table, data, preferred_element_type=jnp.float32, precision=lax.Pr...  6.98 us
    all_to_all x1, starting transfers between devices, body(): lax.all_to_all(g_lesser, 'energy', split_axis=3, concat_axis=1, tiled=True)  6.5 us
    all_to_all x1, starting transfers between devices, convolve(): lax.all_to_all(polar_piece, 'energy', split_axis=1, concat_axis=3, tiled=...  4.92 us
  transfers between devices with their start and end apart: 6, of which 4 were waited for; matrix products, arithmetic and copies ran while one was open for 14% of the time, Pallas kernels for 0%

commit v1 on v0

v1 whole, which is shorter than its diff:
```python
import functools
import math

import jax
import jax.numpy as jnp
from jax import lax
from jax.experimental import pallas as pl
from jax.experimental.pallas import tpu as pltpu
from jax.sharding import PartitionSpec as P

MESH = pl.DeviceIdType.MESH
F32 = jnp.float32
BF16 = jnp.bfloat16


def split(value):
    high = value.astype(BF16)
    return high, (value - high.astype(F32)).astype(BF16)


def product(left, right):
    total = jnp.dot(left[0], right[0], preferred_element_type=F32)
    total += jnp.dot(left[0], right[1], preferred_element_type=F32)
    total += jnp.dot(left[1], right[0], preferred_element_type=F32)
    return total


def kernel(
    n, nc, chunks,
    s_ref, l_ref, g_ref, d_hbm, u_hbm,
    pol_ref, scr_ref,
    gt, lbuf, gbuf, pout, pin, pbuf, pnext, pprev, dbuf, ubuf, uprev, parts,
    l_send, l_recv, g_send, g_recv, p_send, p_recv, c_send, c_recv, u_send, u_recv, in_sem, out_sem,
):
    me = lax.axis_index("energy")
    cell = lax.axis_index("cell")
    size = l_ref.shape[1]
    q4 = n // 4
    quarter, j = me // q4, me % q4
    third = (quarter // 2) * (1 - quarter % 2)
    fourth = (quarter // 2) * (quarter % 2)
    span = size // chunks
    rc = span // q4

    load_d = pltpu.make_async_copy(d_hbm, dbuf, in_sem.at[0])
    load_u = pltpu.make_async_copy(u_hbm, ubuf, in_sem.at[1])
    load_d.start()
    load_u.start()

    barrier = pltpu.get_barrier_semaphore()

    def greet(i, _):
        pl.semaphore_signal(barrier, inc=1, device_id=((me + i) % n, cell), device_id_type=MESH)
        return 0

    lax.fori_loop(1, n, greet, 0)

    @pl.when(cell > 0)
    def _():
        pl.semaphore_signal(barrier, inc=1, device_id=(me, cell - 1), device_id_type=MESH)

    @pl.when(cell < nc - 1)
    def _():
        pl.semaphore_signal(barrier, inc=1, device_id=(me, cell + 1), device_id_type=MESH)

    for part in range(2):
        gt[part] = g_ref[part].T

    pl.semaphore_wait(barrier, n - 1 + jnp.minimum(cell, 1) + jnp.minimum(nc - 1 - cell, 1))

    def near(k):
        return pl.ds(k * rc, rc)

    def far(k, row_owner):
        return pl.ds(pl.multiple_of(k * span + row_owner * rc, 8), rc)

    def l_copy(k, to):
        return pltpu.make_async_remote_copy(
            src_ref=l_ref.at[:, far(k, to)],
            dst_ref=lbuf.at[fourth * q4 + j, :, near(k)],
            send_sem=l_send.at[k, to],
            recv_sem=l_recv.at[k, fourth * q4 + j],
            device_id=((quarter - fourth) * q4 + to, cell),
            device_id_type=MESH,
        )

    def g_copy(k, step, to):
        return pltpu.make_async_remote_copy(
            src_ref=gt.at[:, far(k, to)],
            dst_ref=gbuf.at[me, :, near(k)],
            send_sem=g_send.at[k, step, to],
            recv_sem=g_recv.at[k, me],
            device_id=((quarter + step - fourth) * q4 + to, cell),
            device_id_type=MESH,
        )

    def p_copy(k, w):
        return pltpu.make_async_remote_copy(
            src_ref=pout.at[w, :, near(k)],
            dst_ref=pin.at[quarter, :, far(k, j)],
            send_sem=p_send.at[k, w],
            recv_sem=p_recv.at[k, quarter, j],
            device_id=(w, cell),
            device_id_type=MESH,
        )

    def landed(ref, sem):
        pltpu.make_async_copy(ref, ref, sem).wait()

    g_steps = (3 - quarter) * (1 - quarter // 2) + third + fourth

    for k in range(chunks):

        def send_g(i, _, k=k):
            step, to = g_steps - 1 - i // q4, (j + i) % q4

            @pl.when((quarter + step - fourth) * q4 + to != me)
            def _():
                g_copy(k, step, to).start()

            return 0

        lax.fori_loop(0, g_steps * q4, send_g, 0)

        def send_l(i, _, k=k):
            to = (j + i) % q4

            @pl.when((quarter - fourth) * q4 + to != me)
            def _():
                l_copy(k, to).start()

            return 0

        lax.fori_loop(0, q4, send_l, 0)

    @pl.when(quarter < 3)
    def _():
        for k in range(chunks):
            lbuf[j, :, near(k)] = l_ref[:, far(k, j)]
            gbuf[me, :, near(k)] = gt[:, far(k, j)]

    load_u.wait()
    ubuf[...] = ubuf[...] * (s_ref[0].astype(F32) * 0.125)

    def u_copy():
        return pltpu.make_async_remote_copy(
            src_ref=ubuf, dst_ref=uprev, send_sem=u_send, recv_sem=u_recv,
            device_id=(me, cell + 1), device_id_type=MESH,
        )

    load_d.wait()

    def prepare(slot, ref, turn):
        for part in range(2):
            value = ref[part]
            flipped = value.T
            forward = flipped if turn else value
            backward = value if turn else flipped
            parts[slot, part, 0], parts[slot, part, 1] = split(forward)
            parts[slot, 2 + part, 0], parts[slot, 2 + part, 1] = split(backward)

    prepare(0, dbuf, False)
    prepare(1, ubuf, False)

    @pl.when(cell < nc - 1)
    def _():
        u_copy().start()

    factor = 1.0 / math.sqrt(n)
    depth = q4 * (1 + third) * (1 - fourth)
    shifts = q4 * ((quarter + 1) * (1 - quarter // 2) + 4 * third)

    def compute(k):
        def wait_l(s, _):
            @pl.when(s != j)
            def _():
                landed(lbuf.at[s, :, near(k)], l_recv.at[k, s])

            return 0

        def wait_g(e, _):
            @pl.when(e != me)
            def _():
                landed(gbuf.at[e, :, near(k)], g_recv.at[k, e])

            return 0

        lax.fori_loop(0, depth, wait_l, 0)
        lax.fori_loop(0, shifts, wait_g, 0)

        def one_shift(w, _):
            def add(s, total):
                real, imaginary = total
                e = quarter * q4 + s - w
                lr, li = lbuf[s, 0, near(k)], lbuf[s, 1, near(k)]
                gr, gi = gbuf[e, 0, near(k)], gbuf[e, 1, near(k)]
                return real + (lr * gr - li * gi), imaginary + (lr * gi + li * gr)

            zero = jnp.zeros((rc, size), F32)
            first = jnp.maximum(w - quarter * q4, 0)
            real, imaginary = lax.fori_loop(first, depth, add, (zero, zero))
            pout[w, 0, near(k)] = imaginary * factor
            pout[w, 1, near(k)] = real * (-factor)
            return 0

        lax.fori_loop(0, shifts, one_shift, 0)

        def send_p(w, _):
            @pl.when(w != me)
            def _():
                p_copy(k, w).start()

            @pl.when(w == me)
            def _():
                pin[quarter, :, far(k, j)] = pout[w, :, near(k)]

            return 0

        lax.fori_loop(0, shifts, send_p, 0)

    def neighbour_copy(k, side):
        rows = pl.ds(k * span, span)
        return pltpu.make_async_remote_copy(
            src_ref=pbuf.at[:, rows],
            dst_ref=(pnext if side == 0 else pprev).at[:, rows],
            send_sem=c_send.at[k, side],
            recv_sem=c_recv.at[k, side],
            device_id=(me, cell - 1 if side == 0 else cell + 1),
            device_id_type=MESH,
        )

    def finish(k):
        rows = pl.ds(k * span, span)

        def wait_from(source):
            def wait_p(i, _):
                @pl.when(source * q4 + i != me)
                def _():
                    landed(pin.at[source, :, far(k, i)], p_recv.at[k, source, i])

                return 0

            lax.fori_loop(0, q4, wait_p, 0)

        @pl.when(quarter == 0)
        def _():
            wait_from(0)

        @pl.when(quarter <= 1)
        def _():
            wait_from(1)

        wait_from(2)

        @pl.when(quarter == 0)
        def _():
            pbuf[:, rows] = pin[0, :, rows] + pin[1, :, rows] + pin[2, :, rows]

        @pl.when(quarter == 1)
        def _():
            pbuf[:, rows] = pin[1, :, rows] + pin[2, :, rows]

        @pl.when(quarter >= 2)
        def _():
            pbuf[:, rows] = pin[2, :, rows]

        @pl.when(cell > 0)
        def _():
            neighbour_copy(k, 0).start()

        @pl.when(cell < nc - 1)
        def _():
            neighbour_copy(k, 1).start()

        pltpu.make_async_copy(pbuf.at[:, rows], pol_ref.at[:, rows], out_sem.at[k]).start()

    for k in range(chunks):
        compute(k)
        if k == 0:

            @pl.when(cell > 0)
            def _():
                landed(uprev, u_recv)
                prepare(2, uprev, True)

        if k > 0:
            finish(k - 1)
    finish(chunks - 1)

    def term(slot, ref):
        def pair(part):
            return parts[slot, part, 0], parts[slot, part, 1]

        p_real, p_imag = split(ref[0]), split(ref[1])
        mid_real = split(product(pair(0), p_real) - product(pair(1), p_imag))
        mid_imag = split(product(pair(0), p_imag) + product(pair(1), p_real))
        real = product(mid_real, pair(2)) + product(mid_imag, pair(3))
        imaginary = product(mid_imag, pair(2)) - product(mid_real, pair(3))
        return real, imaginary

    scr_ref[0], scr_ref[1] = term(0, pbuf)

    @pl.when(cell < nc - 1)
    def _():
        for k in range(chunks):
            landed(pnext.at[:, pl.ds(k * span, span)], c_recv.at[k, 0])
        real, imaginary = term(1, pnext)
        scr_ref[0] += real
        scr_ref[1] += imaginary

    @pl.when(cell > 0)
    def _():
        for k in range(chunks):
            landed(pprev.at[:, pl.ds(k * span, span)], c_recv.at[k, 1])
        real, imaginary = term(2, pprev)
        scr_ref[0] += real
        scr_ref[1] += imaginary

    for k in range(chunks):
        rows = pl.ds(k * span, span)

        def end_g(i, _, k=k):
            step, to = i // q4, i % q4

            @pl.when((quarter + step - fourth) * q4 + to != me)
            def _():
                g_copy(k, step, to).wait_send()

            return 0

        lax.fori_loop(0, g_steps * q4, end_g, 0)

        def end_l(to, _, k=k):
            @pl.when((quarter - fourth) * q4 + to != me)
            def _():
                l_copy(k, to).wait_send()

            return 0

        lax.fori_loop(0, q4, end_l, 0)

        def end_p(w, _, k=k):
            @pl.when(w != me)
            def _():
                p_copy(k, w).wait_send()

            return 0

        lax.fori_loop(0, shifts, end_p, 0)

        @pl.when(cell > 0)
        def _():
            neighbour_copy(k, 0).wait_send()

        @pl.when(cell < nc - 1)
        def _():
            neighbour_copy(k, 1).wait_send()

        pltpu.make_async_copy(pbuf.at[:, rows], pol_ref.at[:, rows], out_sem.at[k]).wait()

    @pl.when(cell < nc - 1)
    def _():
        u_copy().wait_send()


def body(n, nc, g_lesser, g_greater, w_diag, w_upper, coupled):
    size = g_lesser.shape[-1]
    shape = g_lesser.shape
    q4 = n // 4
    chunks = max(1, min(4, size // (8 * q4)))
    rows = size // q4
    block = (2, size, size)
    vmem = pl.BlockSpec(memory_space=pltpu.VMEM)
    anywhere = pl.BlockSpec(memory_space=pl.ANY)
    dma = pltpu.SemaphoreType.DMA
    out = pl.pallas_call(
        functools.partial(kernel, n, nc, chunks),
        out_shape=(jax.ShapeDtypeStruct(block, F32), jax.ShapeDtypeStruct(block, F32)),
        in_specs=[pl.BlockSpec(memory_space=pltpu.SMEM), vmem, vmem, anywhere, anywhere],
        out_specs=(anywhere, vmem),
        scratch_shapes=[
            pltpu.VMEM(block, F32),
            pltpu.VMEM((2 * q4, 2, rows, size), F32),
            pltpu.VMEM((n, 2, rows, size), F32),
            pltpu.VMEM((n, 2, rows, size), F32),
            pltpu.VMEM((3,) + block, F32),
            pltpu.VMEM(block, F32),
            pltpu.VMEM(block, F32),
            pltpu.VMEM(block, F32),
            pltpu.VMEM(block, F32),
            pltpu.VMEM(block, F32),
            pltpu.VMEM(block, F32),
            pltpu.VMEM((3, 4, 2, size, size), BF16),
            dma((chunks, q4)),
            dma((chunks, 2 * q4)),
            dma((chunks, 3, q4)),
            dma((chunks, n)),
            dma((chunks, n)),
            dma((chunks, 3, q4)),
            dma((chunks, 2)),
            dma((chunks, 2)),
            dma(()),
            dma(()),
            dma((2,)),
            dma((chunks,)),
        ],
        compiler_params=pltpu.CompilerParams(
            collective_id=0, has_side_effects=True, vmem_limit_bytes=48 * 1024 * 1024
        ),
    )(
        coupled,
        g_lesser.reshape(block),
        g_greater.reshape(block),
        w_diag.reshape(block),
        w_upper.reshape(block),
    )
    return tuple(array.reshape(shape) for array in out)


def solution(mesh):
    spec = P(None, "energy", "cell", None, None)
    return jax.shard_map(
        functools.partial(body, mesh.shape["energy"], mesh.shape["cell"]),
        mesh=mesh,
        in_specs=(spec, spec, spec, spec, P("cell")),
        out_specs=(spec, spec),
        check_vma=False,
    )
```

time: 91.6 us -> 70.1 us (0.77)
  Pallas kernels: 0 us -> 62.4 us
  waiting for transfers between devices: 35.1 us -> 0 us
  starting transfers between devices: 27.2 us -> 0 us
  matrix products: 18.8 us -> 0 us
  other arithmetic: 1.77 us -> 0 us
    pallas_call x0 -> x1, Pallas kernels: none -> 62.4 us  [body(): pl.pallas_call(functools.partial(kernel, n, nc, chunks), out_shape=(jax.S...]
    all_to_all x3 -> x0, waiting for transfers between devices: 31.6 us -> none  [the longest x1 12.4 us: body(): lax.all_to_all(g_lesser, 'energy', split_axis=3, concat_axis=1, tiled=True)]
    dot_general x36 -> x0, matrix products: 18.8 us -> none  [the longest x24 11.9 us: matmul(): jnp.einsum('...ij,...jk->...ik', first, second, precision=lax.Precision.H...]
    all_to_all x3 -> x0, starting transfers between devices: 16.3 us -> none  [the longest x1 6.5 us: body(): lax.all_to_all(g_lesser, 'energy', split_axis=3, concat_axis=1, tiled=True)]
    ppermute x3 -> x0, starting transfers between devices: 10.9 us -> none  [shifted(): return lax.ppermute(shard, axis, pairs)]
    ppermute x3 -> x0, waiting for transfers between devices: 3.51 us -> none  [shifted(): return lax.ppermute(shard, axis, pairs)]
    slice x3 -> x0, local copies, waits for them, and re-layouts: 2.7 us -> none  [the longest x1 1.34 us: convolve(): lesser_flat[0]]
    unnamed x10, local copies, waits for them, and re-layouts: 3.3 us -> 5.75 us
  transfers between devices with their start and end apart: 6 -> 0, of which waited for: 4 -> 0; matrix products, arithmetic and copies ran while one was open for 14% -> 0% of each run, Pallas kernels for 0% -> 0%
where the time goes in v1:
time: 70.1 us; the launch traced here: 69.4 us
  Pallas kernels  62.4 us (89%)
  local copies, waits for them, and re-layouts  5.75 us (8%)
  between operations  1.3 us (2%)
    pallas_call x1, Pallas kernels, body(): pl.pallas_call(functools.partial(kernel, n, nc, chunks), out_shape=(jax.S...  62.4 us
    unnamed x10, local copies, waits for them, and re-layouts  5.75 us

profile of v1, /device:TPU:1, one launch (start us, length us, event | category | flops | bytes accessed | tf_op | source)
XLA Modules:
  0.0 69.4 jit_solution(11521398920372533423)
XLA Ops:
  1.3 0.0 copy-start
  1.3 1.0 %copy-done = f32[2,1,1,256,256]{4,3,2,1,0:T(8,128)S(1)} copy-done((f32[2,1,1,256,256]{4,3,2,1,0:T(8,128)S(1)}, f32[2,1,1,256,256]{4,3,2,1,0:T(8,128)}, u32[]{:S(2)}) %copy-start) | copy-done | bytes 524312
  2.3 0.0 copy-start.1
  2.3 1.0 %copy-done.1 = f32[2,1,1,256,256]{4,3,2,1,0:T(8,128)S(1)} copy-done((f32[2,1,1,256,256]{4,3,2,1,0:T(8,128)S(1)}, f32[2,1,1,256,256]{4,3,2,1,0:T(8,128)}, u32[]{:S(2)}) %copy-start.1) | copy-done | bytes 524312
  3.4 0.0 copy-start.2
  3.4 1.0 %copy-done.2 = f32[2,1,1,256,256]{4,3,2,1,0:T(8,128)S(1)} copy-done((f32[2,1,1,256,256]{4,3,2,1,0:T(8,128)S(1)}, f32[2,1,1,256,256]{4,3,2,1,0:T(8,128)}, u32[]{:S(2)}) %copy-start.2) | copy-done | bytes 524312
  4.4 0.0 copy-start.3
  4.4 1.0 %copy-done.3 = f32[2,1,1,256,256]{4,3,2,1,0:T(8,128)S(1)} copy-done((f32[2,1,1,256,256]{4,3,2,1,0:T(8,128)S(1)}, f32[2,1,1,256,256]{4,3,2,1,0:T(8,128)}, u32[]{:S(2)}) %copy-start.3) | copy-done | bytes 524312
  5.4 62.4 %shard_map.68 = (f32[2,256,256]{2,1,0:T(8,128)S(1)}, f32[2,256,256]{2,1,0:T(8,128)S(1)}) custom-call(s32[1]{0:T(128)S(6)} %copy.11.s_ref, f32[2,256,256]{2,1,0:T(8,128)S(1)} %bitcast.10, f32[2,256,256]{2,1,0:T(8,128)S(1)} %bitcast.11, f32[2,256,256]{2,1,0:T(8,128)S(1)} %bitcast.12, f32[2,256,256]{2,1,0:T(8,128)S(1)} %bitcast.13), custom_call_target="tpu_custom_call" | custom-call | tf_op jit(solution)/shard_map/pallas_call | solution.py:376
  67.8 0.8 %copy.12 = f32[2,1,1,256,256]{4,3,2,1,0:T(8,128)} copy(f32[2,1,1,256,256]{4,3,2,1,0:T(8,128)S(1)} %bitcast.15) | data formatting | bytes 1048576
  68.6 0.8 %copy.13 = f32[2,1,1,256,256]{4,3,2,1,0:T(8,128)} copy(f32[2,1,1,256,256]{4,3,2,1,0:T(8,128)S(1)} %bitcast.14) | data formatting | bytes 1048576
Async XLA Ops:
  1.3 1.0 %copy-start = (f32[2,1,1,256,256]{4,3,2,1,0:T(8,128)S(1)}, f32[2,1,1,256,256]{4,3,2,1,0:T(8,128)}, u32[]{:S(2)}) copy-start(f32[2,1,1,256,256]{4,3,2,1,0:T(8,128)} %param.5) | copy-start | bytes 1572868
  2.3 1.0 %copy-start.1 = (f32[2,1,1,256,256]{4,3,2,1,0:T(8,128)S(1)}, f32[2,1,1,256,256]{4,3,2,1,0:T(8,128)}, u32[]{:S(2)}) copy-start(f32[2,1,1,256,256]{4,3,2,1,0:T(8,128)} %param.6) | copy-start | bytes 1572868
  3.4 1.0 %copy-start.2 = (f32[2,1,1,256,256]{4,3,2,1,0:T(8,128)S(1)}, f32[2,1,1,256,256]{4,3,2,1,0:T(8,128)}, u32[]{:S(2)}) copy-start(f32[2,1,1,256,256]{4,3,2,1,0:T(8,128)} %param.7) | copy-start | bytes 1572868
  4.4 1.0 %copy-start.3 = (f32[2,1,1,256,256]{4,3,2,1,0:T(8,128)S(1)}, f32[2,1,1,256,256]{4,3,2,1,0:T(8,128)}, u32[]{:S(2)}) copy-start(f32[2,1,1,256,256]{4,3,2,1,0:T(8,128)} %param.8) | copy-start | bytes 1572868

commit v2 on v1

v2 whole, which is shorter than its diff:
```python
import functools
import math

import jax
import jax.numpy as jnp
from jax import lax
from jax.experimental import pallas as pl
from jax.experimental.pallas import tpu as pltpu
from jax.sharding import PartitionSpec as P

MESH = pl.DeviceIdType.MESH
F32 = jnp.float32
BF16 = jnp.bfloat16


def split(value):
    high = value.astype(BF16)
    return high, (value - high.astype(F32)).astype(BF16)


def product(left, right):
    total = jnp.dot(left[0], right[0], preferred_element_type=F32)
    total += jnp.dot(left[0], right[1], preferred_element_type=F32)
    total += jnp.dot(left[1], right[0], preferred_element_type=F32)
    return total


def kernel(
    n, nc, chunks,
    s_ref, l_hbm, g_hbm, d_hbm, u_hbm,
    pol_ref, scr_ref,
    graw, gt, lbuf, gbuf, pout, pslab, psum, pbuf, pnext, pprev, dbuf, ubuf, uprev, parts,
    l_send, l_recv, g_send, g_recv, b_send, b_recv, lb_send, lb_recv,
    p_send, p_recv, d_send, d_recv, c_send, c_recv, u_send, u_recv, in_sem, own_sem, out_sem,
):
    me = lax.axis_index("energy")
    cell = lax.axis_index("cell")
    size = l_hbm.shape[1]
    q4 = n // 4
    quarter, j = me // q4, me % q4
    third = (quarter // 2) * (1 - quarter % 2)
    fourth = (quarter // 2) * (quarter % 2)
    span = size // chunks
    rc = span // q4

    def near(k):
        return pl.ds(k * rc, rc)

    def far(k, row_owner):
        return pl.ds(pl.multiple_of(k * span + row_owner * rc, 8), rc)

    def own_copy(k):
        return pltpu.make_async_copy(l_hbm.at[:, far(k, j)], lbuf.at[j, :, near(k)], own_sem.at[k])

    load_g = pltpu.make_async_copy(g_hbm, graw, in_sem.at[2])
    load_d = pltpu.make_async_copy(d_hbm, dbuf, in_sem.at[0])
    load_u = pltpu.make_async_copy(u_hbm, ubuf, in_sem.at[1])
    load_g.start()

    barrier = pltpu.get_barrier_semaphore()

    def greet(i, _):
        pl.semaphore_signal(barrier, inc=1, device_id=((me + i) % n, cell), device_id_type=MESH)
        return 0

    lax.fori_loop(1, n, greet, 0)

    @pl.when(cell > 0)
    def _():
        pl.semaphore_signal(barrier, inc=1, device_id=(me, cell - 1), device_id_type=MESH)

    @pl.when(cell < nc - 1)
    def _():
        pl.semaphore_signal(barrier, inc=1, device_id=(me, cell + 1), device_id_type=MESH)

    load_d.start()
    load_u.start()
    for k in range(chunks):
        own_copy(k).start()
    load_g.wait()
    for part in range(2):
        gt[part] = graw[part].T

    pl.semaphore_wait(barrier, n - 1 + jnp.minimum(cell, 1) + jnp.minimum(nc - 1 - cell, 1))

    def remote(src, dst, send, recv, energy):
        return pltpu.make_async_remote_copy(
            src_ref=src, dst_ref=dst, send_sem=send, recv_sem=recv,
            device_id=(energy, cell), device_id_type=MESH,
        )

    def l_copy(k, to):
        return remote(
            l_hbm.at[:, far(k, to)], lbuf.at[j, :, near(k)],
            l_send.at[k, to], l_recv.at[k, j], quarter * q4 + to,
        )

    def g_copy(k, to):
        return remote(
            gt.at[:, far(k, to)], gbuf.at[me, :, near(k)],
            g_send.at[k, to], g_recv.at[k, j], quarter * q4 + to,
        )

    def slab(k, step):
        ref = gbuf.at[pl.ds(quarter * q4, q4), :, near(k)]
        return remote(
            ref, ref, b_send.at[k, step + 1], b_recv.at[k, quarter], (quarter + step) * q4 + j
        )

    def l_slab(k):
        return remote(
            lbuf.at[pl.ds(0, q4), :, near(k)], lbuf.at[pl.ds(q4, q4), :, near(k)],
            lb_send.at[k], lb_recv.at[k], (quarter - 1) * q4 + j,
        )

    def p_copy(k, target):
        return remote(
            pout.at[pl.ds(target * q4, q4), :, near(k)], pslab.at[quarter, :, :, near(k)],
            p_send.at[k, target], p_recv.at[k, quarter], target * q4 + j,
        )

    def d_copy(k, to):
        return remote(
            psum.at[to, :, near(k)], pbuf.at[:, far(k, j)],
            d_send.at[k, to], d_recv.at[k, j], quarter * q4 + to,
        )

    def landed(ref, sem):
        pltpu.make_async_copy(ref, ref, sem).wait()

    for k in range(chunks):

        def spread(i, _, k=k):
            to = (j + i) % q4
            g_copy(k, to).start()
            l_copy(k, to).start()
            return 0

        lax.fori_loop(1, q4, spread, 0)

    for k in range(chunks):
        gbuf[me, :, near(k)] = gt[:, far(k, j)]

    def relay(k):
        own_copy(k).wait()

        def arrive(i, _):
            source = (j + i) % q4
            landed(gbuf.at[quarter * q4 + source, :, near(k)], g_recv.at[k, source])
            landed(lbuf.at[source, :, near(k)], l_recv.at[k, source])
            return 0

        lax.fori_loop(1, q4, arrive, 0)

        @pl.when(quarter == 0)
        def _():
            slab(k, 2).start()

        @pl.when(quarter <= 1)
        def _():
            slab(k, 1).start()

        @pl.when(quarter == 3)
        def _():
            slab(k, -1).start()
            l_slab(k).start()

    relay(0)

    load_u.wait()
    ubuf[...] = ubuf[...] * (s_ref[0].astype(F32) * 0.125)

    def u_copy():
        return pltpu.make_async_remote_copy(
            src_ref=ubuf, dst_ref=uprev, send_sem=u_send, recv_sem=u_recv,
            device_id=(me, cell + 1), device_id_type=MESH,
        )

    load_d.wait()

    def prepare(slot, ref, turn):
        for part in range(2):
            value = ref[part]
            flipped = value.T
            forward = flipped if turn else value
            backward = value if turn else flipped
            parts[slot, part, 0], parts[slot, part, 1] = split(forward)
            parts[slot, 2 + part, 0], parts[slot, 2 + part, 1] = split(backward)

    prepare(0, dbuf, False)
    if chunks > 1:
        relay(1)
    prepare(1, ubuf, False)

    @pl.when(cell < nc - 1)
    def _():
        u_copy().start()

    factor = 1.0 / math.sqrt(n)
    depth = q4 * (1 + third) * (1 - fourth)
    shifts = q4 * ((quarter + 1) * (1 - quarter // 2) + 4 * third)

    def wait_slab(k, source):
        landed(gbuf.at[pl.ds(source * q4, q4), :, near(k)], b_recv.at[k, source])

    def compute(k):
        @pl.when(quarter == 1)
        def _():
            wait_slab(k, 0)

        @pl.when(quarter == 2)
        def _():
            for source in (0, 1, 3):
                wait_slab(k, source)
            landed(lbuf.at[pl.ds(q4, q4), :, near(k)], lb_recv.at[k])

        def one_shift(w, _):
            def add(s, total):
                real, imaginary = total
                e = quarter * q4 + s - w
                lr, li = lbuf[s, 0, near(k)], lbuf[s, 1, near(k)]
                gr, gi = gbuf[e, 0, near(k)], gbuf[e, 1, near(k)]
                return real + (lr * gr - li * gi), imaginary + (lr * gi + li * gr)

            zero = jnp.zeros((rc, size), F32)
            first = jnp.maximum(w - quarter * q4, 0)
            real, imaginary = lax.fori_loop(first, depth, add, (zero, zero))
            pout[w, 0, near(k)] = imaginary * factor
            pout[w, 1, near(k)] = real * (-factor)
            return 0

        lax.fori_loop(0, shifts, one_shift, 0)

        @pl.when(quarter == 1)
        def _():
            p_copy(k, 0).start()

        @pl.when(quarter == 2)
        def _():
            for target in (0, 1, 3):
                p_copy(k, target).start()

    def combine(k):
        rows = near(k)

        @pl.when(quarter == 0)
        def _():
            landed(pslab.at[1, :, :, rows], p_recv.at[k, 1])

        @pl.when(quarter != 2)
        def _():
            landed(pslab.at[2, :, :, rows], p_recv.at[k, 2])

        def one(i, _):
            @pl.when(quarter == 0)
            def _():
                psum[i, :, rows] = pout[i, :, rows] + pslab[1, i, :, rows] + pslab[2, i, :, rows]

            @pl.when(quarter == 1)
            def _():
                psum[i, :, rows] = pout[q4 + i, :, rows] + pslab[2, i, :, rows]

            @pl.when(quarter == 2)
            def _():
                psum[i, :, rows] = pout[2 * q4 + i, :, rows]

            @pl.when(quarter == 3)
            def _():
                psum[i, :, rows] = pslab[2, i, :, rows]

            return 0

        lax.fori_loop(0, q4, one, 0)

        def spread(i, _):
            d_copy(k, (j + i) % q4).start()
            return 0

        lax.fori_loop(1, q4, spread, 0)
        pbuf[:, far(k, j)] = psum[j, :, rows]

    def neighbour_copy(k, side):
        rows = pl.ds(k * span, span)
        return pltpu.make_async_remote_copy(
            src_ref=pbuf.at[:, rows],
            dst_ref=(pnext if side == 0 else pprev).at[:, rows],
            send_sem=c_send.at[k, side],
            recv_sem=c_recv.at[k, side],
            device_id=(me, cell - 1 if side == 0 else cell + 1),
            device_id_type=MESH,
        )

    def finish(k):
        rows = pl.ds(k * span, span)

        def arrive(i, _):
            source = (j + i) % q4
            landed(pbuf.at[:, far(k, source)], d_recv.at[k, source])
            return 0

        lax.fori_loop(1, q4, arrive, 0)

        @pl.when(cell > 0)
        def _():
            neighbour_copy(k, 0).start()

        @pl.when(cell < nc - 1)
        def _():
            neighbour_copy(k, 1).start()

        pltpu.make_async_copy(pbuf.at[:, rows], pol_ref.at[:, rows], out_sem.at[k]).start()

    for k in range(chunks + 2):
        if k + 2 < chunks:
            relay(k + 2)
        if k < chunks:
            compute(k)
        if k == 0:

            @pl.when(cell > 0)
            def _():
                landed(uprev, u_recv)
                prepare(2, uprev, True)

        if 1 <= k <= chunks:
            combine(k - 1)
        if k >= 2:
            finish(k - 2)

    def term(slot, ref):
        def pair(part):
            return parts[slot, part, 0], parts[slot, part, 1]

        p_real, p_imag = split(ref[0]), split(ref[1])
        mid_real = split(product(pair(0), p_real) - product(pair(1), p_imag))
        mid_imag = split(product(pair(0), p_imag) + product(pair(1), p_real))
        real = product(mid_real, pair(2)) + product(mid_imag, pair(3))
        imaginary = product(mid_imag, pair(2)) - product(mid_real, pair(3))
        return real, imaginary

    scr_ref[0], scr_ref[1] = term(0, pbuf)

    @pl.when(cell < nc - 1)
    def _():
        for k in range(chunks):
            landed(pnext.at[:, pl.ds(k * span, span)], c_recv.at[k, 0])
        real, imaginary = term(1, pnext)
        scr_ref[0] += real
        scr_ref[1] += imaginary

    @pl.when(cell > 0)
    def _():
        for k in range(chunks):
            landed(pprev.at[:, pl.ds(k * span, span)], c_recv.at[k, 1])
        real, imaginary = term(2, pprev)
        scr_ref[0] += real
        scr_ref[1] += imaginary

    for k in range(chunks):
        rows = pl.ds(k * span, span)

        def ended(i, _, k=k):
            to = (j + i) % q4
            g_copy(k, to).wait_send()
            l_copy(k, to).wait_send()
            d_copy(k, to).wait_send()
            return 0

        lax.fori_loop(1, q4, ended, 0)

        @pl.when(quarter == 0)
        def _(k=k):
            slab(k, 2).wait_send()

        @pl.when(quarter <= 1)
        def _(k=k):
            slab(k, 1).wait_send()

        @pl.when(quarter == 3)
        def _(k=k):
            slab(k, -1).wait_send()
            l_slab(k).wait_send()

        @pl.when(quarter == 1)
        def _(k=k):
            p_copy(k, 0).wait_send()

        @pl.when(quarter == 2)
        def _(k=k):
            for target in (0, 1, 3):
                p_copy(k, target).wait_send()

        @pl.when(cell > 0)
        def _(k=k):
            neighbour_copy(k, 0).wait_send()

        @pl.when(cell < nc - 1)
        def _(k=k):
            neighbour_copy(k, 1).wait_send()

        pltpu.make_async_copy(pbuf.at[:, rows], pol_ref.at[:, rows], out_sem.at[k]).wait()

    @pl.when(cell < nc - 1)
    def _():
        u_copy().wait_send()


def body(n, nc, g_lesser, g_greater, w_diag, w_upper, coupled):
    size = g_lesser.shape[-1]
    shape = g_lesser.shape
    q4 = n // 4
    chunks = max(1, min(4, size // (8 * q4)))
    rows = size // q4
    block = (2, size, size)
    vmem = pl.BlockSpec(memory_space=pltpu.VMEM)
    anywhere = pl.BlockSpec(memory_space=pl.ANY)
    dma = pltpu.SemaphoreType.DMA
    out = pl.pallas_call(
        functools.partial(kernel, n, nc, chunks),
        out_shape=(jax.ShapeDtypeStruct(block, F32), jax.ShapeDtypeStruct(block, F32)),
        in_specs=[pl.BlockSpec(memory_space=pltpu.SMEM)] + [anywhere] * 4,
        out_specs=(anywhere, vmem),
        scratch_shapes=[
            pltpu.VMEM(block, F32),
            pltpu.VMEM(block, F32),
            pltpu.VMEM((2 * q4, 2, rows, size), F32),
            pltpu.VMEM((n, 2, rows, size), F32),
            pltpu.VMEM((n, 2, rows, size), F32),
            pltpu.VMEM((3, q4, 2, rows, size), F32),
            pltpu.VMEM((q4, 2, rows, size), F32),
            pltpu.VMEM(block, F32),
            pltpu.VMEM(block, F32),
            pltpu.VMEM(block, F32),
            pltpu.VMEM(block, F32),
            pltpu.VMEM(block, F32),
            pltpu.VMEM(block, F32),
            pltpu.VMEM((3, 4, 2, size, size), BF16),
            dma((chunks, q4)),
            dma((chunks, q4)),
            dma((chunks, q4)),
            dma((chunks, q4)),
            dma((chunks, 4)),
            dma((chunks, 4)),
            dma((chunks,)),
            dma((chunks,)),
            dma((chunks, 4)),
            dma((chunks, 3)),
            dma((chunks, q4)),
            dma((chunks, q4)),
            dma((chunks, 2)),
            dma((chunks, 2)),
            dma(()),
            dma(()),
            dma((3,)),
            dma((chunks,)),
            dma((chunks,)),
        ],
        compiler_params=pltpu.CompilerParams(
            collective_id=0, has_side_effects=True, vmem_limit_bytes=66000000
        ),
    )(
        coupled,
        g_lesser.reshape(block),
        g_greater.reshape(block),
        w_diag.reshape(block),
        w_upper.reshape(block),
    )
    return tuple(array.reshape(shape) for array in out)


def solution(mesh):
    spec = P(None, "energy", "cell", None, None)
    return jax.shard_map(
        functools.partial(body, mesh.shape["energy"], mesh.shape["cell"]),
        mesh=mesh,
        in_specs=(spec, spec, spec, spec, P("cell")),
        out_specs=(spec, spec),
        check_vma=False,
    )
```

time: 70.1 us -> 57.6 us (0.82)
  Pallas kernels: 62.4 us -> 53.4 us
  local copies, waits for them, and re-layouts: 5.75 us -> 2.72 us
    pallas_call x1, Pallas kernels: 62.4 us -> 53.4 us  [body(): pl.pallas_call(functools.partial(kernel, n, nc, chunks), out_shape=(jax.S...]
    unnamed x10 -> x4, local copies, waits for them, and re-layouts: 5.75 us -> 2.72 us
where the time goes in v2:
time: 57.6 us; the launch traced here: 57.4 us
  Pallas kernels  53.4 us (93%)
  local copies, waits for them, and re-layouts  2.72 us (5%)
  between operations  1.29 us (2%)
    pallas_call x1, Pallas kernels, body(): pl.pallas_call(functools.partial(kernel, n, nc, chunks), out_shape=(jax.S...  53.4 us
    unnamed x4, local copies, waits for them, and re-layouts  2.72 us

profile of v2, /device:TPU:1, one launch (start us, length us, event | category | flops | bytes accessed | tf_op | source)
XLA Modules:
  0.0 57.4 jit_solution(2479651106387294978)
XLA Ops:
  1.3 53.4 %shard_map.68 = (f32[2,256,256]{2,1,0:T(8,128)}, f32[2,256,256]{2,1,0:T(8,128)}) custom-call(s32[1]{0:T(128)S(6)} %copy.11.s_ref, f32[2,256,256]{2,1,0:T(8,128)} %bitcast.10, f32[2,256,256]{2,1,0:T(8,128)} %bitcast.11, f32[2,256,256]{2,1,0:T(8,128)} %bitcast.12, f32[2,256,256]{2,1,0:T(8,128)} %bitcast.13), custom_call_target="tpu_custom_call" | custom-call | tf_op jit(solution)/shard_map/pallas_call | solution.py:418
  54.7 0.0 copy-start
  54.7 1.9 %copy.12 = f32[2,1,1,256,256]{4,3,2,1,0:T(8,128)} copy(f32[2,1,1,256,256]{4,3,2,1,0:T(8,128)} %bitcast.15) | data formatting | bytes 1048576
  56.6 0.0 copy-done
  56.6 0.8 %copy.13 = f32[2,1,1,256,256]{4,3,2,1,0:T(8,128)} copy(f32[2,1,1,256,256]{4,3,2,1,0:T(8,128)S(1)} %bitcast.14) | data formatting | bytes 1048576
Async XLA Ops:
  54.7 1.9 %copy-start = (f32[2,256,256]{2,1,0:T(8,128)S(1)}, f32[2,256,256]{2,1,0:T(8,128)}, u32[]{:S(2)}) copy-start(f32[2,256,256]{2,1,0:T(8,128)} %get-tuple-element.5) | copy-start | bytes 1572868

commit v3 on v2

--- a/solution.py
+++ b/solution.py
@@ -29,7 +29,7 @@
     n, nc, chunks,
     s_ref, l_hbm, g_hbm, d_hbm, u_hbm,
     pol_ref, scr_ref,
-    graw, gt, lbuf, gbuf, pout, pslab, psum, pbuf, pnext, pprev, dbuf, ubuf, uprev, parts,
+    graw, gt, lbuf, gbuf, pout, pslab, psum, pbuf, pnext, pprev, dbuf, ubuf, uprev, parts, mid,
     l_send, l_recv, g_send, g_recv, b_send, b_recv, lb_send, lb_recv,
     p_send, p_recv, d_send, d_recv, c_send, c_recv, u_send, u_recv, in_sem, own_sem, out_sem,
 ):
@@ -310,6 +310,37 @@
 
         pltpu.make_async_copy(pbuf.at[:, rows], pol_ref.at[:, rows], out_sem.at[k]).start()
 
+    def pair(slot, part):
+        return parts[slot, part, 0], parts[slot, part, 1]
+
+    def right_product(slot, ref, first, last):
+        rows = pl.ds(first * span, (last - first) * span)
+        p_real, p_imag = split(ref[0, rows]), split(ref[1, rows])
+        real = product(p_real, pair(slot, 2)) + product(p_imag, pair(slot, 3))
+        imaginary = product(p_imag, pair(slot, 2)) - product(p_real, pair(slot, 3))
+        mid[slot, 0, 0, rows], mid[slot, 0, 1, rows] = split(real)
+        mid[slot, 1, 0, rows], mid[slot, 1, 1, rows] = split(imaginary)
+
+    def left_product(slot):
+        m_real, m_imag = (mid[slot, 0, 0], mid[slot, 0, 1]), (mid[slot, 1, 0], mid[slot, 1, 1])
+        real = product(pair(slot, 0), m_real) - product(pair(slot, 1), m_imag)
+        imaginary = product(pair(slot, 0), m_imag) + product(pair(slot, 1), m_real)
+        return real, imaginary
+
+    def from_neighbour(side, first, last, whole):
+        @pl.when(cell < nc - 1 if side == 0 else cell > 0)
+        def _():
+            ref = pnext if side == 0 else pprev
+            for k in range(first, last):
+                landed(ref.at[:, pl.ds(k * span, span)], c_recv.at[k, side])
+            right_product(side + 1, ref, first, last)
+            if whole:
+                real, imaginary = left_product(side + 1)
+                scr_ref[0] += real
+                scr_ref[1] += imaginary
+
+    bounds = sorted({0, chunks // 2, chunks - 1, chunks})
+    batches = list(zip(bounds[:-1], bounds[1:]))
     for k in range(chunks + 2):
         if k + 2 < chunks:
             relay(k + 2)
@@ -326,35 +357,25 @@
             combine(k - 1)
         if k >= 2:
             finish(k - 2)
-
-    def term(slot, ref):
-        def pair(part):
-            return parts[slot, part, 0], parts[slot, part, 1]
-
-        p_real, p_imag = split(ref[0]), split(ref[1])
-        mid_real = split(product(pair(0), p_real) - product(pair(1), p_imag))
-        mid_imag = split(product(pair(0), p_imag) + product(pair(1), p_real))
-        real = product(mid_real, pair(2)) + product(mid_imag, pair(3))
-        imaginary = product(mid_imag, pair(2)) - product(mid_real, pair(3))
-        return real, imaginary
-
-    scr_ref[0], scr_ref[1] = term(0, pbuf)
-
-    @pl.when(cell < nc - 1)
+        for first, last in batches[:-1]:
+            if k == last + 1:
+                right_product(0, pbuf, first, last)
+            if k == last + 2:
+                from_neighbour(0, first, last, False)
+                from_neighbour(1, first, last, False)
+
+    right_product(0, pbuf, *batches[-1])
+    scr_ref[0], scr_ref[1] = left_product(0)
+
+    @pl.when(cell % 2 == 0)
     def _():
-        for k in range(chunks):
-            landed(pnext.at[:, pl.ds(k * span, span)], c_recv.at[k, 0])
-        real, imaginary = term(1, pnext)
-        scr_ref[0] += real
-        scr_ref[1] += imaginary
-
-    @pl.when(cell > 0)
+        from_neighbour(0, *batches[-1], True)
+        from_neighbour(1, *batches[-1], True)
+
+    @pl.when(cell % 2 == 1)
     def _():
-        for k in range(chunks):
-            landed(pprev.at[:, pl.ds(k * span, span)], c_recv.at[k, 1])
-        real, imaginary = term(2, pprev)
-        scr_ref[0] += real
-        scr_ref[1] += imaginary
+        from_neighbour(1, *batches[-1], True)
+        from_neighbour(0, *batches[-1], True)
 
     for k in range(chunks):
         rows = pl.ds(k * span, span)
@@ -409,7 +430,7 @@
     size = g_lesser.shape[-1]
     shape = g_lesser.shape
     q4 = n // 4
-    chunks = max(1, min(4, size // (8 * q4)))
+    chunks = max(1, min(8, size // (8 * q4)))
     rows = size // q4
     block = (2, size, size)
     vmem = pl.BlockSpec(memory_space=pltpu.VMEM)
@@ -435,6 +456,7 @@
             pltpu.VMEM(block, F32),
             pltpu.VMEM(block, F32),
             pltpu.VMEM((3, 4, 2, size, size), BF16),
+            pltpu.VMEM((3, 2, 2, size, size), BF16),
             dma((chunks, q4)),
             dma((chunks, q4)),
             dma((chunks, q4)),

time: 57.6 us -> 54 us (0.938)
  Pallas kernels: 53.4 us -> 49.8 us
    pallas_call x1, Pallas kernels: 53.4 us -> 49.8 us  [body(): pl.pallas_call(functools.partial(kernel, n, nc, chunks), out_shape=(jax.S...]
where the time goes in v3:
time: 54 us; the launch traced here: 53.8 us
  Pallas kernels  49.8 us (92%)
  local copies, waits for them, and re-layouts  2.72 us (5%)
  between operations  1.29 us (2%)
    pallas_call x1, Pallas kernels, body(): pl.pallas_call(functools.partial(kernel, n, nc, chunks), out_shape=(jax.S...  49.8 us
    unnamed x4, local copies, waits for them, and re-layouts  2.72 us

profile of v3, /device:TPU:1, one launch (start us, length us, event | category | flops | bytes accessed | tf_op | source)
XLA Modules:
  0.0 53.8 jit_solution(16214590519035926419)
XLA Ops:
  1.3 49.8 %shard_map.68 = (f32[2,256,256]{2,1,0:T(8,128)}, f32[2,256,256]{2,1,0:T(8,128)}) custom-call(s32[1]{0:T(128)S(6)} %copy.11.s_ref, f32[2,256,256]{2,1,0:T(8,128)} %bitcast.10, f32[2,256,256]{2,1,0:T(8,128)} %bitcast.11, f32[2,256,256]{2,1,0:T(8,128)} %bitcast.12, f32[2,256,256]{2,1,0:T(8,128)} %bitcast.13), custom_call_target="tpu_custom_call" | custom-call | tf_op jit(solution)/shard_map/pallas_call | solution.py:439
  51.1 0.0 copy-start
  51.1 1.9 %copy.12 = f32[2,1,1,256,256]{4,3,2,1,0:T(8,128)} copy(f32[2,1,1,256,256]{4,3,2,1,0:T(8,128)} %bitcast.15) | data formatting | bytes 1048576
  53.0 0.0 copy-done
  53.0 0.8 %copy.13 = f32[2,1,1,256,256]{4,3,2,1,0:T(8,128)} copy(f32[2,1,1,256,256]{4,3,2,1,0:T(8,128)S(1)} %bitcast.14) | data formatting | bytes 1048576
Async XLA Ops:
  51.1 1.9 %copy-start = (f32[2,256,256]{2,1,0:T(8,128)S(1)}, f32[2,256,256]{2,1,0:T(8,128)}, u32[]{:S(2)}) copy-start(f32[2,256,256]{2,1,0:T(8,128)} %get-tuple-element.5) | copy-start | bytes 1572868

commit v4 on v3

--- a/solution.py
+++ b/solution.py
@@ -138,8 +138,21 @@
 
         lax.fori_loop(1, q4, spread, 0)
 
+    load_u.wait()
+    ubuf[...] = ubuf[...] * (s_ref[0].astype(F32) * 0.125)
+
+    def u_copy():
+        return pltpu.make_async_remote_copy(
+            src_ref=ubuf, dst_ref=uprev, send_sem=u_send, recv_sem=u_recv,
+            device_id=(me, cell + 1), device_id_type=MESH,
+        )
+
     for k in range(chunks):
         gbuf[me, :, near(k)] = gt[:, far(k, j)]
+
+    @pl.when(cell < nc - 1)
+    def _():
+        u_copy().start()
 
     def relay(k):
         own_copy(k).wait()
@@ -166,15 +179,6 @@
             l_slab(k).start()
 
     relay(0)
-
-    load_u.wait()
-    ubuf[...] = ubuf[...] * (s_ref[0].astype(F32) * 0.125)
-
-    def u_copy():
-        return pltpu.make_async_remote_copy(
-            src_ref=ubuf, dst_ref=uprev, send_sem=u_send, recv_sem=u_recv,
-            device_id=(me, cell + 1), device_id_type=MESH,
-        )
 
     load_d.wait()
 
@@ -188,13 +192,12 @@
             parts[slot, 2 + part, 0], parts[slot, 2 + part, 1] = split(backward)
 
     prepare(0, dbuf, False)
-    if chunks > 1:
+    ahead = min(4, chunks)
+    if ahead > 1:
         relay(1)
     prepare(1, ubuf, False)
-
-    @pl.when(cell < nc - 1)
-    def _():
-        u_copy().start()
+    for k in range(2, ahead):
+        relay(k)
 
     factor = 1.0 / math.sqrt(n)
     depth = q4 * (1 + third) * (1 - fourth)
@@ -342,11 +345,11 @@
     bounds = sorted({0, chunks // 2, chunks - 1, chunks})
     batches = list(zip(bounds[:-1], bounds[1:]))
     for k in range(chunks + 2):
-        if k + 2 < chunks:
-            relay(k + 2)
+        if k + ahead < chunks:
+            relay(k + ahead)
         if k < chunks:
             compute(k)
-        if k == 0:
+        if k == chunks // 4:
 
             @pl.when(cell > 0)
             def _():

time: 54 us -> 54.3 us (level)
  no operation moved by 1% of the time
where the time goes in v4:
time: 54.3 us; the launch traced here: 54.2 us
  Pallas kernels  50.1 us (92%)
  local copies, waits for them, and re-layouts  2.72 us (5%)
  between operations  1.29 us (2%)
    pallas_call x1, Pallas kernels, body(): pl.pallas_call(functools.partial(kernel, n, nc, chunks), out_shape=(jax.S...  50.1 us
    unnamed x4, local copies, waits for them, and re-layouts  2.72 us

profile of v4, /device:TPU:1, one launch (start us, length us, event | category | flops | bytes accessed | tf_op | source)
XLA Modules:
  0.0 54.2 jit_solution(14944866929268666015)
XLA Ops:
  1.3 50.1 %shard_map.68 = (f32[2,256,256]{2,1,0:T(8,128)}, f32[2,256,256]{2,1,0:T(8,128)}) custom-call(s32[1]{0:T(128)S(6)} %copy.11.s_ref, f32[2,256,256]{2,1,0:T(8,128)} %bitcast.10, f32[2,256,256]{2,1,0:T(8,128)} %bitcast.11, f32[2,256,256]{2,1,0:T(8,128)} %bitcast.12, f32[2,256,256]{2,1,0:T(8,128)} %bitcast.13), custom_call_target="tpu_custom_call" | custom-call | tf_op jit(solution)/shard_map/pallas_call | solution.py:442
  51.4 0.0 copy-start
  51.4 1.9 %copy.12 = f32[2,1,1,256,256]{4,3,2,1,0:T(8,128)} copy(f32[2,1,1,256,256]{4,3,2,1,0:T(8,128)} %bitcast.15) | data formatting | bytes 1048576
  53.4 0.0 copy-done
  53.4 0.8 %copy.13 = f32[2,1,1,256,256]{4,3,2,1,0:T(8,128)} copy(f32[2,1,1,256,256]{4,3,2,1,0:T(8,128)S(1)} %bitcast.14) | data formatting | bytes 1048576
Async XLA Ops:
  51.4 1.9 %copy-start = (f32[2,256,256]{2,1,0:T(8,128)S(1)}, f32[2,256,256]{2,1,0:T(8,128)}, u32[]{:S(2)}) copy-start(f32[2,256,256]{2,1,0:T(8,128)} %get-tuple-element.5) | copy-start | bytes 1572868

commit v5 on v3

--- a/solution.py
+++ b/solution.py
@@ -196,7 +196,6 @@
     def _():
         u_copy().start()
 
-    factor = 1.0 / math.sqrt(n)
     depth = q4 * (1 + third) * (1 - fourth)
     shifts = q4 * ((quarter + 1) * (1 - quarter // 2) + 4 * third)
 
@@ -225,8 +224,8 @@
             zero = jnp.zeros((rc, size), F32)
             first = jnp.maximum(w - quarter * q4, 0)
             real, imaginary = lax.fori_loop(first, depth, add, (zero, zero))
-            pout[w, 0, near(k)] = imaginary * factor
-            pout[w, 1, near(k)] = real * (-factor)
+            pout[w, 0, near(k)] = imaginary
+            pout[w, 1, near(k)] = -real
             return 0
 
         lax.fori_loop(0, shifts, one_shift, 0)
@@ -487,7 +486,8 @@
         w_diag.reshape(block),
         w_upper.reshape(block),
     )
-    return tuple(array.reshape(shape) for array in out)
+    factor = 1.0 / math.sqrt(n)
+    return tuple(array.reshape(shape) * factor for array in out)
 
 
 def solution(mesh):

time: 54 us -> 53.5 us (level)
  local copies, waits for them, and re-layouts: 2.72 us -> 0 us
  other arithmetic: 0 us -> 2.28 us
    unnamed x4 -> x0, local copies, waits for them, and re-layouts: 2.72 us -> none
    unnamed x0 -> x1, other arithmetic: none -> 2.28 us
where the time goes in v5:
time: 53.5 us; the launch traced here: 53.4 us
  Pallas kernels  49.8 us (93%)
  other arithmetic  2.28 us (4%)
  between operations  1.29 us (2%)
    pallas_call x1, Pallas kernels, body(): pl.pallas_call(functools.partial(kernel, n, nc, chunks), out_shape=(jax.S...  49.8 us
    unnamed x1, other arithmetic  2.28 us

profile of v5, /device:TPU:1, one launch (start us, length us, event | category | flops | bytes accessed | tf_op | source)
XLA Modules:
  0.0 53.4 jit_solution(9152402349875988264)
XLA Ops:
  1.3 49.8 %shard_map.68 = (f32[2,256,256]{2,1,0:T(8,128)}, f32[2,256,256]{2,1,0:T(8,128)}) custom-call(s32[1]{0:T(128)S(6)} %copy.9.s_ref, f32[2,256,256]{2,1,0:T(8,128)} %bitcast.12, f32[2,256,256]{2,1,0:T(8,128)} %bitcast.13, f32[2,256,256]{2,1,0:T(8,128)} %bitcast.14, f32[2,256,256]{2,1,0:T(8,128)} %bitcast.15), custom_call_target="tpu_custom_call" | custom-call | tf_op jit(solution)/shard_map/pallas_call | solution.py:438
  51.1 2.3 %multiply_bitcast_fusion = (f32[2,1,1,256,256]{4,3,2,1,0:T(8,128)}, f32[2,1,1,256,256]{4,3,2,1,0:T(8,128)}) fusion(f32[2,256,256]{2,1,0:T(8,128)} %get-tuple-element.5, f32[2,256,256]{2,1,0:T(8,128)} %get-tuple-element.4), kind=kLoop, calls=%fused_computation | loop fusion | flops 262144 | bytes 2097152
